TPU v7x, 512 devices: a whole 4x4x16 slice. The times are simulated.
512 devices in a mesh: sp: 64 (over x_lo, z, core), hd: 8 (over y, x_hi).
Axes of the slice: x: 4 (x_hi: 2, x_lo: 2; x = x_hi * 2 + x_lo), y: 4, z: 16, core: 2. Of those that a mesh axis runs over, the one named last changes fastest.
Arguments:
- stream: bfloat16 [3, 8, 64, 5120], P(None, 'hd', 'sp'), may hold values from -6 to 6
- queries: bfloat16 [3, 8, 64, 5120], P(None, None, 'sp', 'hd'), may hold values from -40 to 40
- span_k: bfloat16 [3, 8, 64, 5120], P(None, None, 'sp', 'hd'), may hold values from -40 to 40
- span_v: bfloat16 [3, 8, 64, 5120], P(None, None, 'sp', 'hd'), may hold values from -6 to 6
- cache_k: bfloat16 [6144, 5120], P('sp', 'hd'), may hold values from -6 to 6
- cache_v: bfloat16 [6144, 5120], P('sp', 'hd'), may hold values from -6 to 6
- cache_age: int32 [6144], P('sp'), may hold values from 0 to 20, as said below
- history: int32 [1], replicated, may hold values from 1 to 20
- out_weight: bfloat16 [5120, 5120], P('hd', 'sp'), may hold values from -2 to 2
- attn_gate: float32 [5120], replicated, may hold values from 0.5 to 1.5
- head_shift: float32 [5120], replicated, may hold values from -3 to 3
- head_scale: float32 [5120], replicated, may hold values from -1.75 to 1.75
- head_weight: bfloat16 [5120, 64], replicated, may hold values from -0.078125 to 0.078125
- latent_cache: bfloat16 [2, 16, 128, 16], P(None, 'hd', 'sp'), may hold values from -6 to 6
- conv_weight: bfloat16 [432, 384], replicated, may hold values from -0.3125 to 0.3125
- rms_gain: float32 [384], replicated, may hold values from 0.25 to 1.75
Outputs:
- stream_out: bfloat16 [3, 8, 64, 5120], P(None, 'hd', 'sp')
- decoded: bfloat16 [3, 16, 128, 384], P(None, 'hd', 'sp')
Inputs may be any that keep to these rules, and one draw needn't show every extreme that they name: `cache_age`: 20 marks an empty cache slot. Among the 96 slots of each index of sp the live ones come first and number at least 24; some index of sp has all its slots live.
All inputs are finite; a program needn't handle non-finite values.
Results may differ from a plain program's by a relative error of at most 0.017.
Values may be sent and summed in bfloat16 or wider, within the bound.
No kernel may reach another device: no remote copies, remote signals or barrier semaphores. Data moves between devices by JAX's collectives and lax.ppermute only.
A program may use at most 64 MiB of HBM per device.

v0:
```python
import math
import jax
import jax.numpy as jnp
from jax import lax
from jax.sharding import PartitionSpec as P

HDIM = 128
LAT = 16
PATCH = 2


def padded_2(cells, sides, width):
    for axis, dim in sides:
        count = lax.axis_size(axis)
        ends = count - 1
        head = lax.slice_in_dim(cells, 0, width, axis=dim)
        tail = lax.slice_in_dim(cells, cells.shape[dim] - width, cells.shape[dim], axis=dim)
        cells = jnp.concatenate(
            [
                lax.ppermute(tail, axis, [(i, (i + 1) % count) for i in range(ends)]),
                cells,
                lax.ppermute(head, axis, [((i + 1) % count, i) for i in range(ends)]),
            ],
            axis=dim,
        )
    return cells


def head_partials(head_index, all_queries, all_keys, all_values, is_valid):
    offset = head_index * HDIM
    query_part = lax.dynamic_slice_in_dim(all_queries, offset, HDIM, 1)
    key_part = lax.dynamic_slice_in_dim(all_keys, offset, HDIM, 1)
    value_part = lax.dynamic_slice_in_dim(all_values, offset, HDIM, 1)
    scores = lax.dot_general(
        query_part, key_part, (((1,), (1,)), ((), ())), preferred_element_type=jnp.float32
    )
    scores = jnp.where(is_valid[None, :], scores * (1.0 / math.sqrt(HDIM)), -1e30)
    top_score = jnp.max(scores, axis=1)
    weights = jnp.exp(scores - top_score[:, None]).astype(jnp.bfloat16)
    weight_sum = jnp.sum(weights.astype(jnp.float32), axis=1)
    summed = jnp.dot(weights, value_part, preferred_element_type=jnp.float32)
    return (top_score, weight_sum, summed)


def settle(incoming):
    top_score, weight_sum, summed = incoming
    peak_score = jnp.max(top_score, axis=4, keepdims=True)
    factor = jnp.exp(top_score - peak_score)
    denominator = jnp.sum(weight_sum * factor, axis=4)
    numerator = jnp.sum(summed * factor[..., None], axis=4)
    return numerator / denominator[..., None]


def causal_conv(padded, frames, height, breadth, conv_weight, rms_gain):
    tap_list = []
    for step_t in range(3):
        for step_i in range(3):
            for step_j in range(3):
                tap_list.append(
                    padded[
                        step_t : step_t + frames,
                        step_i : step_i + height,
                        step_j : step_j + breadth,
                        :,
                    ]
                )
    patches = jnp.concatenate(tap_list, axis=-1)
    conv_out = jnp.dot(
        patches.reshape(-1, patches.shape[-1]), conv_weight, preferred_element_type=jnp.float32
    )
    mean_square = jnp.mean(conv_out * conv_out, axis=-1, keepdims=True)
    scaled = conv_out * lax.rsqrt(mean_square + 1e-06) * rms_gain
    return jax.nn.silu(scaled).astype(jnp.bfloat16).reshape(frames, height, breadth, -1)


def local(
    stream,
    queries,
    span_k,
    span_v,
    cache_k,
    cache_v,
    cache_age,
    history,
    out_weight,
    attn_gate,
    head_shift,
    head_scale,
    head_weight,
    latent_cache,
    conv_weight,
    rms_gain,
):
    frames = queries.shape[0]
    row_total = queries.shape[1]
    local_d = queries.shape[3]
    head_count = local_d // HDIM
    gathered = lax.all_gather(queries, "sp", axis=2, tiled=True)
    col_total = gathered.shape[2]
    all_queries = gathered.reshape(-1, local_d)
    all_keys = jnp.concatenate([cache_k, span_k.reshape(-1, local_d)], axis=0)
    all_values = jnp.concatenate([cache_v, span_v.reshape(-1, local_d)], axis=0)
    is_valid = jnp.concatenate([cache_age < history[0], jnp.ones((frames * row_total,), jnp.bool_)])

    def one_head(head_index):
        return head_partials(head_index, all_queries, all_keys, all_values, is_valid)

    top_score, weight_sum, summed = lax.map(one_head, jnp.arange(head_count, dtype=jnp.int32))
    top_parts = top_score.reshape(head_count, frames, row_total, col_total, 1)
    sum_parts = weight_sum.reshape(head_count, frames, row_total, col_total, 1)
    out_parts = summed.reshape(head_count, frames, row_total, col_total, 1, HDIM)
    attended_f = settle(
        (
            lax.all_to_all(top_parts, "sp", split_axis=3, concat_axis=4, tiled=True),
            lax.all_to_all(sum_parts, "sp", split_axis=3, concat_axis=4, tiled=True),
            lax.all_to_all(out_parts, "sp", split_axis=3, concat_axis=4, tiled=True),
        )
    )
    attended = (
        jnp.transpose(attended_f, (1, 2, 3, 0, 4))
        .reshape(frames, row_total, 1, local_d)
        .astype(jnp.bfloat16)
    )
    own_rows = attended.reshape(-1, local_d)
    partial_sum = jnp.dot(
        own_rows,
        lax.all_gather(out_weight, "sp", axis=1, tiled=True),
        preferred_element_type=jnp.float32,
    )
    projected = lax.psum_scatter(
        partial_sum.reshape(frames, row_total, 1, -1).astype(jnp.bfloat16),
        "hd",
        scatter_dimension=1,
        tiled=True,
    ).astype(jnp.float32)
    stream_out = (stream.astype(jnp.float32) + attn_gate * projected).astype(jnp.bfloat16)
    mixed_f = stream_out.astype(jnp.float32)
    centre_mean = jnp.mean(mixed_f, axis=-1, keepdims=True)
    centred = mixed_f - centre_mean
    variance = jnp.mean(centred * centred, axis=-1, keepdims=True)
    normed = (centred * lax.rsqrt(variance + 1e-06) * (1.0 + head_scale) + head_shift).astype(
        jnp.bfloat16
    )
    own_count = normed.shape[1]
    patch_values = jnp.dot(
        normed.reshape(-1, normed.shape[3]), head_weight, preferred_element_type=jnp.float32
    ).astype(jnp.bfloat16)
    patch_values = patch_values.reshape(frames, own_count, 1, PATCH, PATCH, LAT)
    latent = jnp.transpose(patch_values, (0, 1, 3, 2, 4, 5)).reshape(
        frames, own_count * PATCH, PATCH, LAT
    )
    sequence = jnp.concatenate([latent_cache, latent], axis=0)
    padded = padded_2(sequence, (("sp", 2), ("hd", 1)), 1)
    decoded = causal_conv(padded, frames, own_count * PATCH, PATCH, conv_weight, rms_gain)
    return (stream_out, decoded)


def solution(mesh):
    placed = (
        P(None, "hd", "sp", None),
        P(None, None, "sp", "hd"),
        P(None, None, "sp", "hd"),
        P(None, None, "sp", "hd"),
        P("sp", "hd"),
        P("sp", "hd"),
        P("sp"),
        P(),
        P("hd", "sp"),
        P(),
        P(),
        P(),
        P(),
        P(None, "hd", "sp", None),
        P(),
        P(),
    )
    return jax.shard_map(
        local,
        mesh=mesh,
        in_specs=placed,
        out_specs=(P(None, "hd", "sp", None), P(None, "hd", "sp", None)),
        check_vma=False,
    )
```

profile of v0, /device:TPU:6, one launch (start us, length us, event | category | flops | bytes accessed | tf_op | source)
XLA Modules:
  0.0 595.1 jit_solution(1144554674838404245)
XLA Ops:
  7.2 0.7 all-gather.3.cloned.1.call-update
  8.6 0.7 broadcast_compare_fusion
  9.3 1.0 pad_maximum_fusion
  10.3 125.3 %all-gather.3.cloned.1.call-done = bf16[3,8,64,640]{3,1,2,0:T(8,128)(2,1)} async-done(((bf16[3,8,1,640]{3,1,2,0:T(8,128)(2,1)}), bf16[3,8,64,640]{3,1,2,0:T(8,128)(2,1)}) %all-gather.3.cloned.1.call-update) | async-done | bytes 1966096 | tf_op jit(solution)/shard_map/all_gather | solution.py:98
  135.6 1.9 copy.44
  137.5 16.8 %while.14 = (s32[]{:T(128)}, f32[5,1536]{1,0:T(8,128)S(1)}, f32[5,1536]{1,0:T(8,128)S(1)}, f32[5,1536,128]{2,1,0:T(8,128)}, pred[120]{0:T(512)(128)(4,1)S(1)}, /...) while((s32[]{:T(128)}, f32[5,1536]{1,0:T(8,128)S(1)}, ...), condition=%wide.region_3.4_spmd, body=%wide.region_0.3_spmd.sunk | while | flops 96027648 | bytes 3530947 | solution.py:108
  137.5 0.6 dynamic_slice.30
  138.8 0.4 fusion.50
  139.2 1.2 fusion.51
  140.9 0.6 dynamic_slice.30
  142.1 0.4 fusion.50
  142.5 1.2 fusion.51
  144.3 0.6 dynamic_slice.30
  145.5 0.4 fusion.50
  145.9 1.2 fusion.51
  147.6 0.6 dynamic_slice.30
  148.9 0.4 fusion.50
  149.3 1.2 fusion.51
  151.0 0.6 dynamic_slice.30
  152.2 0.4 fusion.50
  152.6 1.2 fusion.51
  154.4 1.1 copy.46
  155.5 9.4 %all-to-all-start.1 = ((f32[5,3,8,64,1]{2,4,1,0,3:T(1,128)}), f32[5,3,8,64,1]{2,4,1,0,3:T(1,128)S(1)}, u32[]{:S(2)}, u32[]{:S(2)}) async-start(f32[5,3,8,64,1]{2,4,1,0,3:T(1,128)} %copy.46), calls=%async_computation.1 | async-start | bytes 983040 | tf_op jit(solution)/shard_map/all_to_all | solution.py:114
  165.0 1.1 copy.50
  166.1 27.0 %all-to-all-done.1 = f32[5,3,8,64,1]{2,4,1,0,3:T(1,128)S(1)} async-done(((f32[5,3,8,64,1]{2,4,1,0,3:T(1,128)}), f32[5,3,8,64,1]{2,4,1,0,3:T(1,128)S(1)}, u32[]{:S(2)}, u32[]{:S(2)}) %all-to-all-start.1) | async-done | bytes 30752 | tf_op jit(solution)/shard_map/all_to_all | solution.py:114
  193.1 7.9 %all-to-all-start.2 = ((f32[5,3,8,64,1]{2,4,1,0,3:T(1,128)}), f32[5,3,8,64,1]{2,4,1,0,3:T(1,128)S(1)}, u32[]{:S(2)}, u32[]{:S(2)}) async-start(f32[5,3,8,64,1]{2,4,1,0,3:T(1,128)} %copy.50), calls=%async_computation.2 | async-start | bytes 983040 | tf_op jit(solution)/shard_map/all_to_all | solution.py:115
  201.1 6.3 %copy.45 = f32[5,3,8,64,1,128]{5,2,1,0,4,3:T(8,128)} copy(f32[5,3,8,64,1,128]{5,3,2,1,0,4:T(8,128)} %bitcast.65) | data formatting | bytes 7864320 | tf_op jit(solution)/shard_map/reshape | solution.py:111
  207.4 21.8 %all-to-all-done.2 = f32[5,3,8,64,1]{2,4,1,0,3:T(1,128)S(1)} async-done(((f32[5,3,8,64,1]{2,4,1,0,3:T(1,128)}), f32[5,3,8,64,1]{2,4,1,0,3:T(1,128)S(1)}, u32[]{:S(2)}, u32[]{:S(2)}) %all-to-all-start.2) | async-done | bytes 30752 | tf_op jit(solution)/shard_map/all_to_all | solution.py:115
  229.2 8.1 %all-to-all-start = ((f32[5,3,8,64,1,128]{5,2,1,0,4,3:T(8,128)}), f32[5,3,8,64,1,128]{5,2,1,0,4,3:T(8,128)}, u32[]{:S(2)}, u32[]{:S(2)}) async-start(f32[5,3,8,64,1,128]{5,2,1,0,4,3:T(8,128)} %copy.45), calls=%async_computation | async-start | bytes 7864320 | tf_op jit(solution)/shard_map/all_to_all | solution.py:116
  237.4 0.7 all-gather.5.cloned.1.call-update
  238.1 0.4 copy.47
  238.6 0.4 reduce_max.18
  239.4 0.4 copy.51
  240.0 200.1 %all-to-all-done = f32[5,3,8,64,1,128]{5,2,1,0,4,3:T(8,128)} async-done(((f32[5,3,8,64,1,128]{5,2,1,0,4,3:T(8,128)}), f32[5,3,8,64,1,128]{5,2,1,0,4,3:T(8,128)}, u32[]{:S(2)}, u32[]{:S(2)}) %all-to-all-start) | async-done | bytes 3932192 | tf_op jit(solution)/shard_map/all_to_all | solution.py:116
  440.1 2.7 fusion.15
  442.9 20.5 %all-gather.5.cloned.1.call-done = bf16[640,5120]{0,1:T(8,128)(2,1)} async-done(((bf16[640,80]{0,1:T(8,128)(2,1)}), bf16[640,5120]{0,1:T(8,128)(2,1)}) %all-gather.5.cloned.1.call-update) | async-done | bytes 6553616 | tf_op jit(solution)/shard_map/all_gather | solution.py:127
  463.4 4.7 fusion.12
  468.1 0.9 copy.54
  469.1 1.3 dynamic-slice
  470.4 92.3 %all-reduce.4.cloned.1.call-done = bf16[3,8,1,5120]{3,0,2,1:T(4,128)(2,1)} async-done(((bf16[3,8,1,5120]{3,0,2,1:T(4,128)(2,1)}), bf16[3,8,1,5120]{3,0,2,1:T(4,128)(2,1)}) %all-reduce.4.cloned.1.call-update) | async-done | bytes 245776
  562.7 1.6 convert_reduce_fusion.1
  565.0 1.9 collective-permute-start
  567.0 5.8 collective-permute-start.1
  572.8 1.2 collective-permute-done.1
  574.2 4.9 collective-permute-start.2
  579.1 2.4 collective-permute-start.3
  581.6 5.4 collective-permute-done.3
  588.0 0.6 reshape.197
  (105 shorter events, 5.1 us)
Async XLA Ops:
  7.2 557.4 %copy-start = (bf16[5120,64]{0,1:T(8,128)(2,1)S(1)}, bf16[5120,64]{0,1:T(8,128)(2,1)}, u32[]{:S(2)}) copy-start(bf16[5120,64]{0,1:T(8,128)(2,1)} %param.30) | copy-start | bytes 1966084
  7.2 128.5 %all-gather.3.cloned.1.call-start = ((), (), s32[]{:S(2)}) async-start(), calls=%async_computation.3 | async-start | bytes 1996800 | tf_op jit(solution)/shard_map/all_gather | solution.py:98
  155.5 37.6 %all-to-all-start.1 = ((f32[5,3,8,64,1]{2,4,1,0,3:T(1,128)}), f32[5,3,8,64,1]{2,4,1,0,3:T(1,128)S(1)}, u32[]{:S(2)}, u32[]{:S(2)}) async-start(f32[5,3,8,64,1]{2,4,1,0,3:T(1,128)} %copy.46), calls=%async_computation.1 | async-start | bytes 983040 | tf_op jit(solution)/shard_map/all_to_all | solution.py:114
  193.1 36.1 %all-to-all-start.2 = ((f32[5,3,8,64,1]{2,4,1,0,3:T(1,128)}), f32[5,3,8,64,1]{2,4,1,0,3:T(1,128)S(1)}, u32[]{:S(2)}, u32[]{:S(2)}) async-start(f32[5,3,8,64,1]{2,4,1,0,3:T(1,128)} %copy.50), calls=%async_computation.2 | async-start | bytes 983040 | tf_op jit(solution)/shard_map/all_to_all | solution.py:115
  229.2 210.9 %all-to-all-start = ((f32[5,3,8,64,1,128]{5,2,1,0,4,3:T(8,128)}), f32[5,3,8,64,1,128]{5,2,1,0,4,3:T(8,128)}, u32[]{:S(2)}, u32[]{:S(2)}) async-start(f32[5,3,8,64,1,128]{5,2,1,0,4,3:T(8,128)} %copy.45), calls=%async_computation | async-start | bytes 7864320 | tf_op jit(solution)/shard_map/all_to_all | solution.py:116
  237.3 226.1 %all-gather.5.cloned.1.call-start = ((), (), s32[]{:S(2)}) async-start(), calls=%async_computation.4 | async-start | bytes 6656000 | tf_op jit(solution)/shard_map/all_gather | solution.py:127
  238.1 324.6 %all-reduce.4.cloned.1.call-start = ((), (), s32[]{:S(2)}) async-start(), calls=%async_computation.5 | async-start | bytes 655360
  442.8 26.2 %copy-start.7 = (bf16[2,2,2,16]{3,2,1,0:T(2,128)(2,1)S(1)}, bf16[2,2,2,16]{3,2,1,0:T(2,128)(2,1)}, u32[]{:S(2)}) copy-start(bf16[2,2,2,16]{3,2,1,0:T(2,128)(2,1)} %param.31) | copy-start | bytes 772
  442.8 27.5 %copy-start.5 = (f32[5120]{0:T(1024)S(1)}, f32[5120]{0:T(1024)}, u32[]{:S(2)}) copy-start(f32[5120]{0:T(1024)} %param.29) | copy-start | bytes 61444
  442.9 119.8 %copy-start.3 = (bf16[3,1,1,5120]{3,0,2,1:T(4,128)(2,1)S(1)}, bf16[3,1,1,5120]{3,0,2,1:T(4,128)(2,1)}, u32[]{:S(2)}) copy-start(bf16[3,1,1,5120]{3,0,2,1:T(4,128)(2,1)} %param.18) | copy-start | bytes 92164
  442.9 119.8 %copy-start.4 = (f32[5120]{0:T(1024)S(1)}, f32[5120]{0:T(1024)}, u32[]{:S(2)}) copy-start(f32[5120]{0:T(1024)} %param.27) | copy-start | bytes 61444
  442.9 121.7 %copy-start.8 = (f32[5120]{0:T(1024)S(1)}, f32[5120]{0:T(1024)}, u32[]{:S(2)}) copy-start(f32[5120]{0:T(1024)} %param.28) | copy-start | bytes 61444
  442.9 144.7 %copy-start.1 = (bf16[432,384]{1,0:T(8,128)(2,1)S(1)}, bf16[432,384]{1,0:T(8,128)(2,1)}, u32[]{:S(2)}) copy-start(bf16[432,384]{1,0:T(8,128)(2,1)} %param.32) | copy-start | bytes 995332
  442.9 145.0 %copy-start.6 = (f32[384]{0:T(512)S(1)}, f32[384]{0:T(512)}, u32[]{:S(2)}) copy-start(f32[384]{0:T(512)} %param.33) | copy-start | bytes 4612
  564.3 24.3 %copy-start.2 = (bf16[3,1,1,5120]{3,0,2,1:T(4,128)(2,1)}, bf16[3,1,1,5120]{3,0,2,1:T(4,128)(2,1)S(1)}, u32[]{:S(2)}) copy-start(bf16[3,1,1,5120]{3,0,2,1:T(4,128)(2,1)S(1)} %get-tuple-element.77) | copy-start | bytes 92164
  565.0 7.8 %collective-permute-start = (bf16[5,2,1,16]{3,2,1,0:T(2,128)(2,1)S(1)}, bf16[5,2,1,16]{3,2,1,0:T(2,128)(2,1)S(1)}, u32[]{:S(2)}, u32[]{:S(2)}) collective-permute-start(bf16[5,2,1,16]{3,2,1,0:T(2,128)(2,1)S(1)} %get-tuple-element.113), channel_id=1, source_target_pairs={{0,8},{8,16},{16,24},{24,32},{32,40},{40,48},{48,56},{56,64},{64,7... | collective-permute-start | bytes 968 | tf_op jit(solution)/shard_map/ppermute | solution.py:20
  567.0 7.1 %collective-permute-start.1 = (bf16[5,2,1,16]{3,2,1,0:T(2,128)(2,1)S(1)}, bf16[5,2,1,16]{3,2,1,0:T(2,128)(2,1)S(1)}, u32[]{:S(2)}, u32[]{:S(2)}) collective-permute-start(bf16[5,2,1,16]{3,2,1,0:T(2,128)(2,1)S(1)} %get-tuple-element.114), channel_id=1, source_target_pairs={{8,0},{16,8},{24,16},{32,24},{40,32},{48,40},{56,48},{64,56},{72,6... | collective-permute-start | bytes 968 | tf_op jit(solution)/shard_map/ppermute | solution.py:22
  574.2 7.5 %collective-permute-start.2 = (bf16[5,1,4,16]{3,2,1,0:T(4,128)(2,1)S(1)}, bf16[5,1,4,16]{3,2,1,0:T(4,128)(2,1)S(1)}, u32[]{:S(2)}, u32[]{:S(2)}) collective-permute-start(bf16[5,1,4,16]{3,2,1,0:T(4,128)(2,1)S(1)} %get-tuple-element.107), channel_id=1, source_target_pairs={{0,1},{1,2},{2,3},{3,4},{4,5},{5,6},{6,7},{8,9},{9,10},{10,11},{11... | collective-permute-start | bytes 1928 | tf_op jit(solution)/shard_map/ppermute | solution.py:20
  579.1 7.9 %collective-permute-start.3 = (bf16[5,1,4,16]{3,2,1,0:T(4,128)(2,1)S(1)}, bf16[5,1,4,16]{3,2,1,0:T(4,128)(2,1)S(1)}, u32[]{:S(2)}, u32[]{:S(2)}) collective-permute-start(bf16[5,1,4,16]{3,2,1,0:T(4,128)(2,1)S(1)} %get-tuple-element.106), channel_id=1, source_target_pairs={{1,0},{2,1},{3,2},{4,3},{5,4},{6,5},{7,6},{9,8},{10,9},{11,10},{12... | collective-permute-start | bytes 1928 | tf_op jit(solution)/shard_map/ppermute | solution.py:22
Sparse Core Ops, SparseCore 0:
  10.1 125.4 all-gather.2
  240.3 223.0 all-gather.4
  469.2 93.4 all-reduce.3
where the time goes:
time: 596 us; the launch traced here: 595 us
  waiting for transfers between devices  495 us (83%)
  starting transfers between devices  40.6 us (7%)
  local copies, waits for them, and re-layouts  20 us (3%)
  between operations  14.8 us (2%)
  matrix products  13.4 us (2%)
  other arithmetic  7.78 us (1%)
    all_to_all x1, waiting for transfers between devices, local(): lax.all_to_all(out_parts, 'sp', split_axis=3, concat_axis=4, tiled=True)  200 us
    all_gather x1, waiting for transfers between devices, local(): gathered = lax.all_gather(queries, 'sp', axis=2, tiled=True)  125 us
    unnamed x4, waiting for transfers between devices  93.7 us
    all_to_all x1, waiting for transfers between devices, local(): lax.all_to_all(top_parts, 'sp', split_axis=3, concat_axis=4, tiled=True)  27 us
    all_to_all x1, waiting for transfers between devices, local(): lax.all_to_all(sum_parts, 'sp', split_axis=3, concat_axis=4, tiled=True)  21.8 us
    all_gather x1, waiting for transfers between devices, local(): lax.all_gather(out_weight, 'sp', axis=1, tiled=True)  20.5 us
  transfers between devices with their start and end apart: 10, of which 8 were waited for; matrix products, arithmetic and copies ran while one was open for 3% of the time, Pallas kernels for 0%

commit v1 on v0

--- a/solution.py
+++ b/solution.py
@@ -95,7 +95,9 @@
     row_total = queries.shape[1]
     local_d = queries.shape[3]
     head_count = local_d // HDIM
-    gathered = lax.all_gather(queries, "sp", axis=2, tiled=True)
+    gathered = jnp.concatenate(
+        lax.all_to_all(jnp.stack([queries] * lax.axis_size("sp")), "sp", 0, 0), axis=2
+    )
     col_total = gathered.shape[2]
     all_queries = gathered.reshape(-1, local_d)
     all_keys = jnp.concatenate([cache_k, span_k.reshape(-1, local_d)], axis=0)

time: 596 us -> 578 us (0.970)
  waiting for transfers between devices: 495 us -> 460 us
  starting transfers between devices: 40.6 us -> 56.8 us
    all_gather x1 -> x0, waiting for transfers between devices: 125 us -> none  [local(): gathered = lax.all_gather(queries, 'sp', axis=2, tiled=True)]
    all_to_all x0 -> x1, waiting for transfers between devices: none -> 90.1 us  [local(): lax.all_to_all(jnp.stack([queries] * lax.axis_size('sp')), 'sp', 0, 0)]
    all_to_all x0 -> x1, starting transfers between devices: none -> 17.4 us  [local(): lax.all_to_all(jnp.stack([queries] * lax.axis_size('sp')), 'sp', 0, 0)]
    unnamed x4 -> x3, waiting for transfers between devices: 93.7 us -> 93.3 us
  transfers between devices with their start and end apart: 10 -> 10, of which waited for: 8 -> 8; matrix products, arithmetic and copies ran while one was open for 3% -> 2% of each run, Pallas kernels for 0% -> 0%
where the time goes in v1:
time: 578 us; the launch traced here: 577 us
  waiting for transfers between devices  460 us (80%)
  starting transfers between devices  56.8 us (10%)
  local copies, waits for them, and re-layouts  22.3 us (4%)
  between operations  15.2 us (3%)
  matrix products  13.4 us (2%)
  other arithmetic  6.14 us (1%)
    all_to_all x1, waiting for transfers between devices, local(): lax.all_to_all(out_parts, 'sp', split_axis=3, concat_axis=4, tiled=True)  200 us
    unnamed x3, waiting for transfers between devices  93.3 us
    all_to_all x1, waiting for transfers between devices, local(): lax.all_to_all(jnp.stack([queries] * lax.axis_size('sp')), 'sp', 0, 0)  90.1 us
    all_to_all x1, waiting for transfers between devices, local(): lax.all_to_all(top_parts, 'sp', split_axis=3, concat_axis=4, tiled=True)  27 us
    all_to_all x1, waiting for transfers between devices, local(): lax.all_to_all(sum_parts, 'sp', split_axis=3, concat_axis=4, tiled=True)  21.8 us
    all_gather x1, waiting for transfers between devices, local(): lax.all_gather(out_weight, 'sp', axis=1, tiled=True)  20.5 us
    all_to_all x1, starting transfers between devices, local(): lax.all_to_all(jnp.stack([queries] * lax.axis_size('sp')), 'sp', 0, 0)  17.4 us
  transfers between devices with their start and end apart: 10, of which 8 were waited for; matrix products, arithmetic and copies ran while one was open for 2% of the time, Pallas kernels for 0%

profile of v1, /device:TPU:6, one launch (start us, length us, event | category | flops | bytes accessed | tf_op | source)
XLA Modules:
  0.0 576.9 jit_solution(8860743462386840622)
XLA Ops:
  7.2 2.2 stack.2
  9.5 17.4 %all-to-all-start = ((bf16[64,3,8,1,640]{4,2,1,3,0:T(8,128)(2,1)}), bf16[64,3,8,1,640]{4,2,1,3,0:T(8,128)(2,1)}, u32[]{:S(2)}, u32[]{:S(2)}) async-start(bf16[64,3,8,1,640]{4,2,1,3,0:T(8,128)(2,1)} %stack.2), calls=%async_computation | async-start | bytes 3932160 | tf_op jit(solution)/shard_map/all_to_all | solution.py:99
  27.7 90.1 %all-to-all-done = bf16[64,3,8,1,640]{4,2,1,3,0:T(8,128)(2,1)} async-done(((bf16[64,3,8,1,640]{4,2,1,3,0:T(8,128)(2,1)}), bf16[64,3,8,1,640]{4,2,1,3,0:T(8,128)(2,1)}, u32[]{:S(2)}, u32[]{:S(2)}) %all-to-all-start) | async-done | bytes 1966112 | tf_op jit(solution)/shard_map/all_to_all | solution.py:99
  117.8 1.9 copy.41
  119.7 16.9 %while.14 = (s32[]{:T(128)}, f32[5,1536]{1,0:T(8,128)S(1)}, f32[5,1536]{1,0:T(8,128)S(1)}, f32[5,1536,128]{2,1,0:T(8,128)}, pred[120]{0:T(512)(128)(4,1)S(1)}, /...) while((s32[]{:T(128)}, f32[5,1536]{1,0:T(8,128)S(1)}, ...), condition=%wide.region_3.4_spmd, body=%wide.region_0.3_spmd.sunk | while | flops 96027648 | bytes 3530947 | solution.py:110
  119.7 0.6 dynamic_slice.30
  120.9 0.4 fusion.50
  121.3 1.2 fusion.51
  123.1 0.6 dynamic_slice.30
  124.3 0.4 fusion.50
  124.7 1.2 fusion.51
  126.5 0.6 dynamic_slice.30
  127.7 0.4 fusion.50
  128.1 1.2 fusion.51
  129.8 0.6 dynamic_slice.30
  131.1 0.4 fusion.50
  131.5 1.2 fusion.51
  133.2 0.6 dynamic_slice.30
  134.4 0.4 fusion.50
  134.9 1.2 fusion.51
  136.7 1.1 copy.43
  137.7 8.3 %all-to-all-start.2 = ((f32[5,3,8,64,1]{2,4,1,0,3:T(1,128)}), f32[5,3,8,64,1]{2,4,1,0,3:T(1,128)S(1)}, u32[]{:S(2)}, u32[]{:S(2)}) async-start(f32[5,3,8,64,1]{2,4,1,0,3:T(1,128)} %copy.43), calls=%async_computation.2 | async-start | bytes 983040 | tf_op jit(solution)/shard_map/all_to_all | solution.py:116
  146.1 1.1 copy.47
  147.2 27.0 %all-to-all-done.2 = f32[5,3,8,64,1]{2,4,1,0,3:T(1,128)S(1)} async-done(((f32[5,3,8,64,1]{2,4,1,0,3:T(1,128)}), f32[5,3,8,64,1]{2,4,1,0,3:T(1,128)S(1)}, u32[]{:S(2)}, u32[]{:S(2)}) %all-to-all-start.2) | async-done | bytes 30752 | tf_op jit(solution)/shard_map/all_to_all | solution.py:116
  174.2 8.0 %all-to-all-start.3 = ((f32[5,3,8,64,1]{2,4,1,0,3:T(1,128)}), f32[5,3,8,64,1]{2,4,1,0,3:T(1,128)S(1)}, u32[]{:S(2)}, u32[]{:S(2)}) async-start(f32[5,3,8,64,1]{2,4,1,0,3:T(1,128)} %copy.47), calls=%async_computation.3 | async-start | bytes 983040 | tf_op jit(solution)/shard_map/all_to_all | solution.py:117
  182.1 6.3 %copy.42 = f32[5,3,8,64,1,128]{5,2,1,0,4,3:T(8,128)} copy(f32[5,3,8,64,1,128]{5,3,2,1,0,4:T(8,128)} %bitcast.68) | data formatting | bytes 7864320 | tf_op jit(solution)/shard_map/reshape | solution.py:113
  188.5 21.8 %all-to-all-done.3 = f32[5,3,8,64,1]{2,4,1,0,3:T(1,128)S(1)} async-done(((f32[5,3,8,64,1]{2,4,1,0,3:T(1,128)}), f32[5,3,8,64,1]{2,4,1,0,3:T(1,128)S(1)}, u32[]{:S(2)}, u32[]{:S(2)}) %all-to-all-start.3) | async-done | bytes 30752 | tf_op jit(solution)/shard_map/all_to_all | solution.py:117
  210.3 8.1 %all-to-all-start.1 = ((f32[5,3,8,64,1,128]{5,2,1,0,4,3:T(8,128)}), f32[5,3,8,64,1,128]{5,2,1,0,4,3:T(8,128)}, u32[]{:S(2)}, u32[]{:S(2)}) async-start(f32[5,3,8,64,1,128]{5,2,1,0,4,3:T(8,128)} %copy.42), calls=%async_computation.1 | async-start | bytes 7864320 | tf_op jit(solution)/shard_map/all_to_all | solution.py:118
  218.5 0.7 all-gather.2.cloned.1.call-update
  219.2 0.4 copy.44
  219.6 0.4 reduce_max.18
  220.5 0.4 copy.48
  221.1 200.2 %all-to-all-done.1 = f32[5,3,8,64,1,128]{5,2,1,0,4,3:T(8,128)} async-done(((f32[5,3,8,64,1,128]{5,2,1,0,4,3:T(8,128)}), f32[5,3,8,64,1,128]{5,2,1,0,4,3:T(8,128)}, u32[]{:S(2)}, u32[]{:S(2)}) %all-to-all-start.1) | async-done | bytes 3932192 | tf_op jit(solution)/shard_map/all_to_all | solution.py:118
  421.3 2.7 fusion.15
  424.1 20.5 %all-gather.2.cloned.1.call-done = bf16[640,5120]{0,1:T(8,128)(2,1)} async-done(((bf16[640,80]{0,1:T(8,128)(2,1)}), bf16[640,5120]{0,1:T(8,128)(2,1)}) %all-gather.2.cloned.1.call-update) | async-done | bytes 6553616 | tf_op jit(solution)/shard_map/all_gather | solution.py:129
  444.6 4.7 fusion.12
  449.3 1.0 copy.51
  450.3 1.3 dynamic-slice
  451.6 92.6 %all-reduce.4.cloned.1.call-done = bf16[3,8,1,5120]{3,0,2,1:T(4,128)(2,1)} async-done(((bf16[3,8,1,5120]{3,0,2,1:T(4,128)(2,1)}), bf16[3,8,1,5120]{3,0,2,1:T(4,128)(2,1)}) %all-reduce.4.cloned.1.call-update) | async-done | bytes 245776
  544.2 1.6 convert_reduce_fusion.1
  546.0 0.3 convolution_convert_fusion
  546.5 1.9 collective-permute-start
  548.4 5.8 collective-permute-start.1
  554.3 1.2 collective-permute-done.1
  555.6 4.9 collective-permute-start.2
  560.6 2.4 collective-permute-start.3
  563.1 5.4 collective-permute-done.3
  569.5 0.6 reshape.200
  (115 shorter events, 4.8 us)
Async XLA Ops:
  7.2 538.9 %copy-start = (bf16[5120,64]{0,1:T(8,128)(2,1)S(1)}, bf16[5120,64]{0,1:T(8,128)(2,1)}, u32[]{:S(2)}) copy-start(bf16[5120,64]{0,1:T(8,128)(2,1)} %param.30) | copy-start | bytes 1966084
  7.2 20.4 %copy-start.13 = (s32[96]{0:T(128)S(1)}, s32[96]{0:T(128)}, u32[]{:S(2)}) copy-start(s32[96]{0:T(128)} %param.24) | copy-start | bytes 1156
  7.2 20.4 %copy-start.6 = (bf16[3,8,1,640]{3,1,2,0:T(8,128)(2,1)S(1)}, bf16[3,8,1,640]{3,1,2,0:T(8,128)(2,1)}, u32[]{:S(2)}) copy-start(bf16[3,8,1,640]{3,1,2,0:T(8,128)(2,1)} %param.20) | copy-start | bytes 92164
  7.2 20.4 %copy-start.7 = (bf16[3,8,1,640]{3,1,2,0:T(8,128)(2,1)S(1)}, bf16[3,8,1,640]{3,1,2,0:T(8,128)(2,1)}, u32[]{:S(2)}) copy-start(bf16[3,8,1,640]{3,1,2,0:T(8,128)(2,1)} %param.21) | copy-start | bytes 92164
  7.2 20.4 %copy-start.3 = (bf16[96,640]{1,0:T(8,128)(2,1)S(1)}, bf16[96,640]{1,0:T(8,128)(2,1)}, u32[]{:S(2)}) copy-start(bf16[96,640]{1,0:T(8,128)(2,1)} %param.22) | copy-start | bytes 368644
  7.2 20.4 %copy-start.4 = (bf16[96,640]{1,0:T(8,128)(2,1)S(1)}, bf16[96,640]{1,0:T(8,128)(2,1)}, u32[]{:S(2)}) copy-start(bf16[96,640]{1,0:T(8,128)(2,1)} %param.23) | copy-start | bytes 368644
  9.5 108.3 %all-to-all-start = ((bf16[64,3,8,1,640]{4,2,1,3,0:T(8,128)(2,1)}), bf16[64,3,8,1,640]{4,2,1,3,0:T(8,128)(2,1)}, u32[]{:S(2)}, u32[]{:S(2)}) async-start(bf16[64,3,8,1,640]{4,2,1,3,0:T(8,128)(2,1)} %stack.2), calls=%async_computation | async-start | bytes 3932160 | tf_op jit(solution)/shard_map/all_to_all | solution.py:99
  137.7 36.4 %all-to-all-start.2 = ((f32[5,3,8,64,1]{2,4,1,0,3:T(1,128)}), f32[5,3,8,64,1]{2,4,1,0,3:T(1,128)S(1)}, u32[]{:S(2)}, u32[]{:S(2)}) async-start(f32[5,3,8,64,1]{2,4,1,0,3:T(1,128)} %copy.43), calls=%async_computation.2 | async-start | bytes 983040 | tf_op jit(solution)/shard_map/all_to_all | solution.py:116
  174.2 36.1 %all-to-all-start.3 = ((f32[5,3,8,64,1]{2,4,1,0,3:T(1,128)}), f32[5,3,8,64,1]{2,4,1,0,3:T(1,128)S(1)}, u32[]{:S(2)}, u32[]{:S(2)}) async-start(f32[5,3,8,64,1]{2,4,1,0,3:T(1,128)} %copy.47), calls=%async_computation.3 | async-start | bytes 983040 | tf_op jit(solution)/shard_map/all_to_all | solution.py:117
  210.3 211.0 %all-to-all-start.1 = ((f32[5,3,8,64,1,128]{5,2,1,0,4,3:T(8,128)}), f32[5,3,8,64,1,128]{5,2,1,0,4,3:T(8,128)}, u32[]{:S(2)}, u32[]{:S(2)}) async-start(f32[5,3,8,64,1,128]{5,2,1,0,4,3:T(8,128)} %copy.42), calls=%async_computation.1 | async-start | bytes 7864320 | tf_op jit(solution)/shard_map/all_to_all | solution.py:118
  218.4 226.2 %all-gather.2.cloned.1.call-start = ((), (), s32[]{:S(2)}) async-start(), calls=%async_computation.4 | async-start | bytes 6656000 | tf_op jit(solution)/shard_map/all_gather | solution.py:129
  219.2 325.0 %all-reduce.4.cloned.1.call-start = ((), (), s32[]{:S(2)}) async-start(), calls=%async_computation.5 | async-start | bytes 655360
  424.0 26.2 %copy-start.11 = (bf16[2,2,2,16]{3,2,1,0:T(2,128)(2,1)S(1)}, bf16[2,2,2,16]{3,2,1,0:T(2,128)(2,1)}, u32[]{:S(2)}) copy-start(bf16[2,2,2,16]{3,2,1,0:T(2,128)(2,1)} %param.31) | copy-start | bytes 772
  424.0 27.5 %copy-start.9 = (f32[5120]{0:T(1024)S(1)}, f32[5120]{0:T(1024)}, u32[]{:S(2)}) copy-start(f32[5120]{0:T(1024)} %param.29) | copy-start | bytes 61444
  424.1 120.1 %copy-start.5 = (bf16[3,1,1,5120]{3,0,2,1:T(4,128)(2,1)S(1)}, bf16[3,1,1,5120]{3,0,2,1:T(4,128)(2,1)}, u32[]{:S(2)}) copy-start(bf16[3,1,1,5120]{3,0,2,1:T(4,128)(2,1)} %param.18) | copy-start | bytes 92164
  424.1 120.1 %copy-start.8 = (f32[5120]{0:T(1024)S(1)}, f32[5120]{0:T(1024)}, u32[]{:S(2)}) copy-start(f32[5120]{0:T(1024)} %param.27) | copy-start | bytes 61444
  424.1 122.0 %copy-start.12 = (f32[5120]{0:T(1024)S(1)}, f32[5120]{0:T(1024)}, u32[]{:S(2)}) copy-start(f32[5120]{0:T(1024)} %param.28) | copy-start | bytes 61444
  424.1 145.0 %copy-start.1 = (bf16[432,384]{1,0:T(8,128)(2,1)S(1)}, bf16[432,384]{1,0:T(8,128)(2,1)}, u32[]{:S(2)}) copy-start(bf16[432,384]{1,0:T(8,128)(2,1)} %param.32) | copy-start | bytes 995332
  424.1 145.3 %copy-start.10 = (f32[384]{0:T(512)S(1)}, f32[384]{0:T(512)}, u32[]{:S(2)}) copy-start(f32[384]{0:T(512)} %param.33) | copy-start | bytes 4612
  545.8 24.3 %copy-start.2 = (bf16[3,1,1,5120]{3,0,2,1:T(4,128)(2,1)}, bf16[3,1,1,5120]{3,0,2,1:T(4,128)(2,1)S(1)}, u32[]{:S(2)}) copy-start(bf16[3,1,1,5120]{3,0,2,1:T(4,128)(2,1)S(1)} %get-tuple-element.77) | copy-start | bytes 92164
  546.5 7.8 %collective-permute-start = (bf16[5,2,1,16]{3,2,1,0:T(2,128)(2,1)S(1)}, bf16[5,2,1,16]{3,2,1,0:T(2,128)(2,1)S(1)}, u32[]{:S(2)}, u32[]{:S(2)}) collective-permute-start(bf16[5,2,1,16]{3,2,1,0:T(2,128)(2,1)S(1)} %get-tuple-element.113), channel_id=1, source_target_pairs={{0,8},{8,16},{16,24},{24,32},{32,40},{40,48},{48,56},{56,64},{64,7... | collective-permute-start | bytes 968 | tf_op jit(solution)/shard_map/ppermute | solution.py:20
  548.4 7.1 %collective-permute-start.1 = (bf16[5,2,1,16]{3,2,1,0:T(2,128)(2,1)S(1)}, bf16[5,2,1,16]{3,2,1,0:T(2,128)(2,1)S(1)}, u32[]{:S(2)}, u32[]{:S(2)}) collective-permute-start(bf16[5,2,1,16]{3,2,1,0:T(2,128)(2,1)S(1)} %get-tuple-element.114), channel_id=1, source_target_pairs={{8,0},{16,8},{24,16},{32,24},{40,32},{48,40},{56,48},{64,56},{72,6... | collective-permute-start | bytes 968 | tf_op jit(solution)/shard_map/ppermute | solution.py:22
  555.6 7.5 %collective-permute-start.2 = (bf16[5,1,4,16]{3,2,1,0:T(4,128)(2,1)S(1)}, bf16[5,1,4,16]{3,2,1,0:T(4,128)(2,1)S(1)}, u32[]{:S(2)}, u32[]{:S(2)}) collective-permute-start(bf16[5,1,4,16]{3,2,1,0:T(4,128)(2,1)S(1)} %get-tuple-element.107), channel_id=1, source_target_pairs={{0,1},{1,2},{2,3},{3,4},{4,5},{5,6},{6,7},{8,9},{9,10},{10,11},{11... | collective-permute-start | bytes 1928 | tf_op jit(solution)/shard_map/ppermute | solution.py:20
  560.6 7.9 %collective-permute-start.3 = (bf16[5,1,4,16]{3,2,1,0:T(4,128)(2,1)S(1)}, bf16[5,1,4,16]{3,2,1,0:T(4,128)(2,1)S(1)}, u32[]{:S(2)}, u32[]{:S(2)}) collective-permute-start(bf16[5,1,4,16]{3,2,1,0:T(4,128)(2,1)S(1)} %get-tuple-element.106), channel_id=1, source_target_pairs={{1,0},{2,1},{3,2},{4,3},{5,4},{6,5},{7,6},{9,8},{10,9},{11,10},{12... | collective-permute-start | bytes 1928 | tf_op jit(solution)/shard_map/ppermute | solution.py:22
Sparse Core Ops, SparseCore 0:
  221.4 223.1 all-gather.1
  450.4 93.7 all-reduce.3
